TPU v7x, 256 devices: a whole 4x4x8 slice. The times are simulated.
256 devices in a mesh: section: 8 (over x, y_hi), dp: 32 (over y_lo, z, core).
Axes of the slice: x: 4, y: 4 (y_hi: 2, y_lo: 2; y = y_hi * 2 + y_lo), z: 8, core: 2. Of those that a mesh axis runs over, the one named last changes fastest.
Arguments:
- latent: bfloat16 [8192, 1536], P('dp'), may hold values from -6 to 6
- target: bfloat16 [8192, 1536], P('dp'), may hold values from -6 to 6
- camera_of_token: int32 [8192], P('dp'), may hold values from 0 to 5
- timestep_indices: int32 [2], replicated, may hold values from 0 to 49
- camera_embedding_table: bfloat16 [6, 1536], replicated, may hold values from -3 to 3
- timestep_embedding_table: bfloat16 [50, 1536], replicated, may hold values from -2.5 to 2.5
- layer_norm_gain: float32 [8, 1536], P('section'), may hold values from 0.25 to 1.75
- frozen_weight: bfloat16 [8, 1536, 1536], P('section', 'dp'), may hold values from -0.15625 to 0.15625
- adapter_down_weight: bfloat16 [8, 64, 1536], P('section'), may hold values from -0.15625 to 0.15625
- adapter_up_weight: bfloat16 [8, 64, 1536], P('section'), may hold values from -0.75 to 0.75
Outputs:
- grad_down: float32 [8, 64, 1536], P('section', None, 'dp')
- grad_up: float32 [8, 64, 1536], P('section', None, 'dp')
Inputs may be any that keep to these rules, and one draw needn't show every extreme that they name: `timestep_indices`: indices of rows of timestep_embedding_table.
All inputs are finite; a program needn't handle non-finite values.
Results may differ from a plain program's by a relative error of at most 0.024.
Values may be sent and summed in bfloat16 or wider, within the bound.
No kernel may reach another device: no remote copies, remote signals or barrier semaphores. Data moves between devices by JAX's collectives and lax.ppermute only.
A program may use at most 64 MiB of HBM per device.

v0:
```python
import math
import jax
import jax.numpy as jnp
from jax import lax
from jax.sharding import PartitionSpec as P

MICRO = 4
BLEND = 0.5
ADAPTER_SCALE = 0.5
EPSILON = 1e-06


def from_behind(block, axis, distance):
    devices = range(lax.axis_size(axis))
    route = [((i - distance) % len(devices), i) for i in devices]
    return lax.ppermute(block, axis, route)


def in_one_piece(arrays, axis, dim, along):
    widths = [a.shape[along] for a in arrays]
    both = jnp.concatenate(arrays, axis=along)
    out = lax.psum_scatter(both, axis, scatter_dimension=dim, tiled=True)
    return tuple(jnp.split(out, [sum(widths[:k]) for k in range(1, len(widths))], axis=along))


def forward_layer_pass(
    hidden_state, layer_weight, down_weight_rows, up_weight_rows, gain_row, modulate_row
):
    hidden_float = hidden_state.astype(jnp.float32)
    inverse_rms = lax.rsqrt(jnp.mean(hidden_float * hidden_float, axis=-1, keepdims=True) + EPSILON)
    normalized_hidden = (hidden_float * inverse_rms * (gain_row * modulate_row)).astype(
        jnp.bfloat16
    )
    low_rank_hidden = lax.dot_general(
        normalized_hidden,
        down_weight_rows,
        (((1,), (1,)), ((), ())),
        preferred_element_type=jnp.float32,
    ).astype(jnp.bfloat16)
    preactivation = jnp.dot(
        normalized_hidden, layer_weight, preferred_element_type=jnp.float32
    ) + ADAPTER_SCALE * jnp.dot(low_rank_hidden, up_weight_rows, preferred_element_type=jnp.float32)
    output = (hidden_float + jax.nn.silu(preactivation)).astype(jnp.bfloat16)
    return (output, normalized_hidden, low_rank_hidden, preactivation)


def backward_layer_pass(
    hidden_state,
    normalized_hidden,
    low_rank_hidden,
    preactivation,
    output_gradient,
    layer_weight,
    down_weight_rows,
    up_weight_rows,
    gain_row,
    modulate_row,
):
    sigmoid_value = jax.nn.sigmoid(preactivation)
    preactivation_gradient = (
        output_gradient * sigmoid_value * (1.0 + preactivation * (1.0 - sigmoid_value))
    ).astype(jnp.bfloat16)
    low_rank_gradient = (
        ADAPTER_SCALE
        * lax.dot_general(
            preactivation_gradient,
            up_weight_rows,
            (((1,), (1,)), ((), ())),
            preferred_element_type=jnp.float32,
        )
    ).astype(jnp.bfloat16)
    norm_grad = lax.dot_general(
        preactivation_gradient,
        layer_weight,
        (((1,), (1,)), ((), ())),
        preferred_element_type=jnp.float32,
    ) + jnp.dot(low_rank_gradient, down_weight_rows, preferred_element_type=jnp.float32)
    up_gradient_term = ADAPTER_SCALE * lax.dot_general(
        low_rank_hidden,
        preactivation_gradient,
        (((0,), (0,)), ((), ())),
        preferred_element_type=jnp.float32,
    )
    down_gradient_term = lax.dot_general(
        low_rank_gradient,
        normalized_hidden,
        (((0,), (0,)), ((), ())),
        preferred_element_type=jnp.float32,
    )
    hidden_float = hidden_state.astype(jnp.float32)
    inverse_rms = lax.rsqrt(jnp.mean(hidden_float * hidden_float, axis=-1, keepdims=True) + EPSILON)
    scaled = hidden_float * inverse_rms
    scaled_grad = norm_grad * (gain_row * modulate_row)
    hidden_gradient = output_gradient + inverse_rms * (
        scaled_grad - scaled * jnp.mean(scaled_grad * scaled, axis=-1, keepdims=True)
    )
    return (hidden_gradient, down_gradient_term, up_gradient_term)


def pick_block(store, first_index, second_index):
    anchor = jnp.zeros((), jnp.int32)
    starts = (first_index, second_index) + (anchor,) * (store.ndim - 2)
    piece = lax.dynamic_slice(store, starts, (1, 1) + store.shape[2:])
    return piece[0, 0]


def place_block(store, value, first_index, second_index):
    anchor = jnp.zeros((), jnp.int32)
    starts = (first_index, second_index) + (anchor,) * (store.ndim - 2)
    return lax.dynamic_update_slice(store, value[None, None], starts)


def local(
    latent,
    target,
    camera_of_token,
    timestep_indices,
    camera_embedding_table,
    timestep_embedding_table,
    layer_norm_gain,
    frozen_weight,
    adapter_down_weight,
    adapter_up_weight,
):
    sections = lax.axis_size("section")
    position = lax.axis_index("section")
    layer_weight = lax.all_gather(frozen_weight[0], "dp", axis=0, tiled=True)
    down_weight_rows = adapter_down_weight[0]
    up_weight_rows = adapter_up_weight[0]
    gain_row = layer_norm_gain[0]
    feature_width = latent.shape[1]
    rank_width = down_weight_rows.shape[0]
    scale_factor = 1.0 / math.sqrt(latent.shape[0] * lax.axis_size("dp"))
    camera_rows = jnp.dot(
        jax.nn.one_hot(camera_of_token, camera_embedding_table.shape[0], dtype=jnp.bfloat16),
        camera_embedding_table,
        preferred_element_type=jnp.float32,
    )
    timestep_modulation = 1.0 + jnp.dot(
        jax.nn.one_hot(timestep_indices, timestep_embedding_table.shape[0], dtype=jnp.bfloat16),
        timestep_embedding_table,
        preferred_element_type=jnp.float32,
    )
    block_count = MICRO
    block_rows = latent.shape[0] // block_count
    latent_blocks = latent.reshape(block_count, block_rows, feature_width)
    target_blocks = target.reshape(block_count, block_rows, feature_width)
    camera_blocks = camera_rows.reshape(block_count, block_rows, feature_width)
    is_first = position == 0
    is_last = position == sections - 1
    tick_total = 2 * sections + block_count - 1
    zero_index = jnp.zeros((), jnp.int32)

    def forward_tick(tick_index, carry):
        offset = tick_index - position
        round_index = (offset >= sections).astype(jnp.int32)
        block_index = offset - round_index * sections
        active = (offset >= 0) & (block_index < block_count)
        safe_block = jnp.clip(block_index, 0, block_count - 1)

        def forward_compute(current):
            (
                received,
                hidden_store,
                normed_store,
                low_store,
                pre_store,
                blend_store,
                adjoint_store,
            ) = current
            latent_block = lax.dynamic_index_in_dim(
                latent_blocks, safe_block, 0, keepdims=False
            ).astype(jnp.float32)
            camera_block = lax.dynamic_index_in_dim(camera_blocks, safe_block, 0, keepdims=False)
            target_block = lax.dynamic_index_in_dim(
                target_blocks, safe_block, 0, keepdims=False
            ).astype(jnp.float32)
            starting = jnp.where(round_index == 0, latent_block, received.astype(jnp.float32))
            first_hidden = (starting + camera_block).astype(jnp.bfloat16)
            hidden_state = jnp.where(is_first, first_hidden, received)
            modulate_row = jnp.where(
                round_index == 0, timestep_modulation[0], timestep_modulation[1]
            )
            output, normalized_hidden, low_rank_hidden, preactivation = forward_layer_pass(
                hidden_state, layer_weight, down_weight_rows, up_weight_rows, gain_row, modulate_row
            )
            hidden_store = place_block(hidden_store, hidden_state, round_index, safe_block)
            normed_store = place_block(normed_store, normalized_hidden, round_index, safe_block)
            low_store = place_block(low_store, low_rank_hidden, round_index, safe_block)
            pre_store = place_block(pre_store, preactivation, round_index, safe_block)
            previous_blend = lax.dynamic_index_in_dim(blend_store, safe_block, 0, keepdims=False)
            previous = jnp.where(round_index == 0, latent_block, previous_blend.astype(jnp.float32))
            blended = BLEND * (previous + output.astype(jnp.float32))
            blend_rounded = blended.astype(jnp.bfloat16)
            keep_blend = jnp.where(round_index == 0, blend_rounded, previous_blend)
            blend_store = lax.dynamic_update_slice(
                blend_store, keep_blend[None], (safe_block, zero_index, zero_index)
            )
            squashed = jnp.tanh(blended)
            adjoint = target_block * (1.0 - squashed * squashed) * scale_factor
            previous_adjoint = lax.dynamic_index_in_dim(
                adjoint_store, safe_block, 0, keepdims=False
            )
            keep_adjoint = jnp.where(round_index == 1, adjoint, previous_adjoint)
            adjoint_store = lax.dynamic_update_slice(
                adjoint_store, keep_adjoint[None], (safe_block, zero_index, zero_index)
            )
            outgoing = jnp.where(is_last, blend_rounded, output)
            return (
                outgoing,
                (hidden_store, normed_store, low_store, pre_store, blend_store, adjoint_store),
            )

        def forward_skip_block(current):
            return (jnp.zeros_like(current[0]), tuple(current[1:]))

        outgoing, stores = lax.cond(active, forward_compute, forward_skip_block, carry)
        incoming = from_behind(outgoing, "section", 1)
        return (incoming,) + tuple(stores)

    forward_start = (
        jnp.zeros((block_rows, feature_width), jnp.bfloat16),
        jnp.zeros((2, block_count, block_rows, feature_width), jnp.bfloat16),
        jnp.zeros((2, block_count, block_rows, feature_width), jnp.bfloat16),
        jnp.zeros((2, block_count, block_rows, rank_width), jnp.bfloat16),
        jnp.zeros((2, block_count, block_rows, feature_width), jnp.float32),
        jnp.zeros((block_count, block_rows, feature_width), jnp.bfloat16),
        jnp.zeros((block_count, block_rows, feature_width), jnp.float32),
    )
    forward_end = lax.fori_loop(0, tick_total, forward_tick, forward_start)
    hidden_store, normed_store, low_store, pre_store, blend_store, adjoint_store = forward_end[1:]
    back_position = sections - 1 - position

    def backward_tick(tick_index, carry):
        offset = tick_index - back_position
        round_back = (offset >= sections).astype(jnp.int32)
        block_index = offset - round_back * sections
        active = (offset >= 0) & (block_index < block_count)
        safe_block = jnp.clip(block_index, 0, block_count - 1)
        forward_round = 1 - round_back

        def backward_compute(current):
            received, down_sum, up_sum = current
            adjoint_block = lax.dynamic_index_in_dim(adjoint_store, safe_block, 0, keepdims=False)
            received_float = received.astype(jnp.float32)
            last_cotangent = jnp.where(
                round_back == 0,
                BLEND * adjoint_block,
                BLEND * (BLEND * adjoint_block + received_float),
            )
            output_gradient = jnp.where(is_last, last_cotangent, received_float)
            hidden_state = pick_block(hidden_store, forward_round, safe_block)
            normalized_hidden = pick_block(normed_store, forward_round, safe_block)
            low_rank_hidden = pick_block(low_store, forward_round, safe_block)
            preactivation = pick_block(pre_store, forward_round, safe_block)
            modulate_row = jnp.where(
                forward_round == 0, timestep_modulation[0], timestep_modulation[1]
            )
            hidden_gradient, down_gradient_term, up_gradient_term = backward_layer_pass(
                hidden_state,
                normalized_hidden,
                low_rank_hidden,
                preactivation,
                output_gradient,
                layer_weight,
                down_weight_rows,
                up_weight_rows,
                gain_row,
                modulate_row,
            )
            return (
                hidden_gradient.astype(jnp.bfloat16),
                down_sum + down_gradient_term,
                up_sum + up_gradient_term,
            )

        def backward_skip_block(current):
            return (jnp.zeros_like(current[0]), current[1], current[2])

        outgoing, down_sum, up_sum = lax.cond(active, backward_compute, backward_skip_block, carry)
        incoming = from_behind(outgoing, "section", -1)
        return (incoming, down_sum, up_sum)

    backward_start = (
        jnp.zeros((block_rows, feature_width), jnp.bfloat16),
        jnp.zeros((rank_width, feature_width), jnp.float32),
        jnp.zeros((rank_width, feature_width), jnp.float32),
    )
    backward_end = lax.fori_loop(0, tick_total, backward_tick, backward_start)
    down_part, up_part = in_one_piece((backward_end[1], backward_end[2]), "dp", 1, 0)
    return (down_part[None], up_part[None])


def solution(mesh):
    in_specs = (
        P("dp", None),
        P("dp", None),
        P("dp"),
        P(),
        P(),
        P(),
        P("section", None),
        P("section", "dp", None),
        P("section", None, None),
        P("section", None, None),
    )
    out_specs = (P("section", None, "dp"), P("section", None, "dp"))
    return jax.shard_map(local, mesh=mesh, in_specs=in_specs, out_specs=out_specs, check_vma=False)
```

profile of v0, /device:TPU:6, one launch (start us, length us, event | category | flops | bytes accessed | tf_op | source)
XLA Modules:
  0.0 969.5 jit_solution(15846906296157261650)
XLA Ops:
  12.0 68.9 %all-gather.3.cloned.1.call-done = bf16[1,1536,1536]{2,1,0:T(8,128)(2,1)} async-done(((bf16[1,48,1536]{2,1,0:T(8,128)(2,1)}), bf16[1,1536,1536]{2,1,0:T(8,128)(2,1)}) %all-gather.3.cloned.1.call-update) | async-done | bytes 4718608 | tf_op jit(solution)/shard_map/all_gather | solution.py:127
  86.8 397.1 %while.42 = (s32[]{:T(128)}, bf16[64,1536]{1,0:T(8,128)(2,1)}, bf16[2,4,64,1536]{3,2,1,0:T(8,128)(2,1)S(1)}, bf16[2,4,64,1536]{3,2,1,0:T(8,128)(2,1)}, bf16[2,4,...) while((s32[]{:T(128)}, bf16[64,1536]{1,0:T(8,128)(2,1)}, ...), condition=%wide.region_4.5_spmd, body=%wide.region_0.4_spmd.sunk | while | flops 332176448 | bytes 21725468 | solution.py:230
  115.6 19.0 %collective-permute-start = (bf16[64,1536]{1,0:T(8,128)(2,1)}, bf16[64,1536]{1,0:T(8,128)(2,1)S(1)}, u32[]{:S(2)}, u32[]{:S(2)}) collective-permute-start(bf16[64,1536]{1,0:T(8,128)(2,1)} %get-tuple-element.1111), channel_id=1, source_target_pairs={{224,0},{0,32},{32,64},{64,96},{96,128},{128,160},{160,192},{192,2... | collective-permute-start | bytes 589832 | tf_op jit(solution)/shard_map/while/body/eval_jaxpr/ppermute | solution.py:16
  139.5 19.0 %collective-permute-start = (bf16[64,1536]{1,0:T(8,128)(2,1)}, bf16[64,1536]{1,0:T(8,128)(2,1)S(1)}, u32[]{:S(2)}, u32[]{:S(2)}) collective-permute-start(bf16[64,1536]{1,0:T(8,128)(2,1)} %get-tuple-element.1111), channel_id=1, source_target_pairs={{224,0},{0,32},{32,64},{64,96},{96,128},{128,160},{160,192},{192,2... | collective-permute-start | bytes 589832 | tf_op jit(solution)/shard_map/while/body/eval_jaxpr/ppermute | solution.py:16
  163.4 19.0 %collective-permute-start = (bf16[64,1536]{1,0:T(8,128)(2,1)}, bf16[64,1536]{1,0:T(8,128)(2,1)S(1)}, u32[]{:S(2)}, u32[]{:S(2)}) collective-permute-start(bf16[64,1536]{1,0:T(8,128)(2,1)} %get-tuple-element.1111), channel_id=1, source_target_pairs={{224,0},{0,32},{32,64},{64,96},{96,128},{128,160},{160,192},{192,2... | collective-permute-start | bytes 589832 | tf_op jit(solution)/shard_map/while/body/eval_jaxpr/ppermute | solution.py:16
  193.3 16.5 %collective-permute-done = bf16[64,1536]{1,0:T(8,128)(2,1)S(1)} collective-permute-done((bf16[64,1536]{1,0:T(8,128)(2,1)}, bf16[64,1536]{1,0:T(8,128)(2,1)S(1)}, u32[]{:S(2)}, u32[]{:S(2)}) %collective-permute-start) | collective-permute-done | bytes 196640 | tf_op jit(solution)/shard_map/while/body/eval_jaxpr/ppermute | solution.py:16
  210.5 13.7 %conditional.4 = (bf16[64,1536]{1,0:T(8,128)(2,1)}, bf16[2,4,64,1536]{3,2,1,0:T(8,128)(2,1)S(1)}, bf16[2,4,64,1536]{3,2,1,0:T(8,128)(2,1)}, bf16[2,4,64,64]{3,2,...) conditional(s32[]{:T(128)} %convert_element_type.177, ...), branch_computations={%region_1.1_spmd, %region_2.3_spmd} | conditional | flops 332176448 | bytes 20152056 | solution.py:217
  233.4 13.7 %conditional.4 = (bf16[64,1536]{1,0:T(8,128)(2,1)}, bf16[2,4,64,1536]{3,2,1,0:T(8,128)(2,1)S(1)}, bf16[2,4,64,1536]{3,2,1,0:T(8,128)(2,1)}, bf16[2,4,64,64]{3,2,...) conditional(s32[]{:T(128)} %convert_element_type.177, ...), branch_computations={%region_1.1_spmd, %region_2.3_spmd} | conditional | flops 332176448 | bytes 20152056 | solution.py:217
  256.7 13.7 %conditional.4 = (bf16[64,1536]{1,0:T(8,128)(2,1)}, bf16[2,4,64,1536]{3,2,1,0:T(8,128)(2,1)S(1)}, bf16[2,4,64,1536]{3,2,1,0:T(8,128)(2,1)}, bf16[2,4,64,64]{3,2,...) conditional(s32[]{:T(128)} %convert_element_type.177, ...), branch_computations={%region_1.1_spmd, %region_2.3_spmd} | conditional | flops 332176448 | bytes 20152056 | solution.py:217
  280.5 13.7 %conditional.4 = (bf16[64,1536]{1,0:T(8,128)(2,1)}, bf16[2,4,64,1536]{3,2,1,0:T(8,128)(2,1)S(1)}, bf16[2,4,64,1536]{3,2,1,0:T(8,128)(2,1)}, bf16[2,4,64,64]{3,2,...) conditional(s32[]{:T(128)} %convert_element_type.177, ...), branch_computations={%region_1.1_spmd, %region_2.3_spmd} | conditional | flops 332176448 | bytes 20152056 | solution.py:217
  330.6 17.2 %collective-permute-start = (bf16[64,1536]{1,0:T(8,128)(2,1)}, bf16[64,1536]{1,0:T(8,128)(2,1)S(1)}, u32[]{:S(2)}, u32[]{:S(2)}) collective-permute-start(bf16[64,1536]{1,0:T(8,128)(2,1)} %get-tuple-element.1111), channel_id=1, source_target_pairs={{224,0},{0,32},{32,64},{64,96},{96,128},{128,160},{160,192},{192,2... | collective-permute-start | bytes 589832 | tf_op jit(solution)/shard_map/while/body/eval_jaxpr/ppermute | solution.py:16
  358.7 13.3 %collective-permute-done = bf16[64,1536]{1,0:T(8,128)(2,1)S(1)} collective-permute-done((bf16[64,1536]{1,0:T(8,128)(2,1)}, bf16[64,1536]{1,0:T(8,128)(2,1)S(1)}, u32[]{:S(2)}, u32[]{:S(2)}) %collective-permute-start) | collective-permute-done | bytes 196640 | tf_op jit(solution)/shard_map/while/body/eval_jaxpr/ppermute | solution.py:16
  372.7 13.7 %conditional.4 = (bf16[64,1536]{1,0:T(8,128)(2,1)}, bf16[2,4,64,1536]{3,2,1,0:T(8,128)(2,1)S(1)}, bf16[2,4,64,1536]{3,2,1,0:T(8,128)(2,1)}, bf16[2,4,64,64]{3,2,...) conditional(s32[]{:T(128)} %convert_element_type.177, ...), branch_computations={%region_1.1_spmd, %region_2.3_spmd} | conditional | flops 332176448 | bytes 20152056 | solution.py:217
  396.6 13.7 %conditional.4 = (bf16[64,1536]{1,0:T(8,128)(2,1)}, bf16[2,4,64,1536]{3,2,1,0:T(8,128)(2,1)S(1)}, bf16[2,4,64,1536]{3,2,1,0:T(8,128)(2,1)}, bf16[2,4,64,64]{3,2,...) conditional(s32[]{:T(128)} %convert_element_type.177, ...), branch_computations={%region_1.1_spmd, %region_2.3_spmd} | conditional | flops 332176448 | bytes 20152056 | solution.py:217
  420.5 13.7 %conditional.4 = (bf16[64,1536]{1,0:T(8,128)(2,1)}, bf16[2,4,64,1536]{3,2,1,0:T(8,128)(2,1)S(1)}, bf16[2,4,64,1536]{3,2,1,0:T(8,128)(2,1)}, bf16[2,4,64,64]{3,2,...) conditional(s32[]{:T(128)} %convert_element_type.177, ...), branch_computations={%region_1.1_spmd, %region_2.3_spmd} | conditional | flops 332176448 | bytes 20152056 | solution.py:217
  444.3 13.7 %conditional.4 = (bf16[64,1536]{1,0:T(8,128)(2,1)}, bf16[2,4,64,1536]{3,2,1,0:T(8,128)(2,1)S(1)}, bf16[2,4,64,1536]{3,2,1,0:T(8,128)(2,1)}, bf16[2,4,64,64]{3,2,...) conditional(s32[]{:T(128)} %convert_element_type.177, ...), branch_computations={%region_1.1_spmd, %region_2.3_spmd} | conditional | flops 332176448 | bytes 20152056 | solution.py:217
  467.6 12.1 %collective-permute-start = (bf16[64,1536]{1,0:T(8,128)(2,1)}, bf16[64,1536]{1,0:T(8,128)(2,1)S(1)}, u32[]{:S(2)}, u32[]{:S(2)}) collective-permute-start(bf16[64,1536]{1,0:T(8,128)(2,1)} %get-tuple-element.1111), channel_id=1, source_target_pairs={{224,0},{0,32},{32,64},{64,96},{96,128},{128,160},{160,192},{192,2... | collective-permute-start | bytes 589832 | tf_op jit(solution)/shard_map/while/body/eval_jaxpr/ppermute | solution.py:16
  485.2 342.2 %while.43 = (s32[]{:T(128)}, bf16[64,1536]{1,0:T(8,128)(2,1)S(1)}, f32[64,1536]{1,0:T(8,128)S(1)}, f32[64,1536]{1,0:T(8,128)S(1)}, s32[]{:T(128)}, /*index=5*/pr...) while((s32[]{:T(128)}, bf16[64,1536]{1,0:T(8,128)(2,1)S(1)}, ...), condition=%wide.region_10.11_spmd, body=%wide.region_5.10_spmd.sunk | while | flops 356265024 | bytes 13259635 | solution.py:289
  485.9 18.9 %collective-permute-done.1 = bf16[64,1536]{1,0:T(8,128)(2,1)S(1)} collective-permute-done((bf16[64,1536]{1,0:T(8,128)(2,1)}, bf16[64,1536]{1,0:T(8,128)(2,1)S(1)}, u32[]{:S(2)}, u32[]{:S(2)}) %collective-permute-start.1) | collective-permute-done | bytes 196640 | tf_op jit(solution)/shard_map/while/body/eval_jaxpr/ppermute | solution.py:16
  591.0 13.7 %collective-permute-start.1 = (bf16[64,1536]{1,0:T(8,128)(2,1)}, bf16[64,1536]{1,0:T(8,128)(2,1)S(1)}, u32[]{:S(2)}, u32[]{:S(2)}) collective-permute-start(bf16[64,1536]{1,0:T(8,128)(2,1)} %get-tuple-element.1134), channel_id=1, source_target_pairs={{32,0},{64,32},{96,64},{128,96},{160,128},{192,160},{224,192},{0,2... | collective-permute-start | bytes 589832 | tf_op jit(solution)/shard_map/while/body/eval_jaxpr/ppermute | solution.py:16
  637.1 15.8 %collective-permute-done.1 = bf16[64,1536]{1,0:T(8,128)(2,1)S(1)} collective-permute-done((bf16[64,1536]{1,0:T(8,128)(2,1)}, bf16[64,1536]{1,0:T(8,128)(2,1)S(1)}, u32[]{:S(2)}, u32[]{:S(2)}) %collective-permute-start.1) | collective-permute-done | bytes 196640 | tf_op jit(solution)/shard_map/while/body/eval_jaxpr/ppermute | solution.py:16
  738.3 13.0 %collective-permute-start.1 = (bf16[64,1536]{1,0:T(8,128)(2,1)}, bf16[64,1536]{1,0:T(8,128)(2,1)S(1)}, u32[]{:S(2)}, u32[]{:S(2)}) collective-permute-start(bf16[64,1536]{1,0:T(8,128)(2,1)} %get-tuple-element.1134), channel_id=1, source_target_pairs={{32,0},{64,32},{96,64},{128,96},{160,128},{192,160},{224,192},{0,2... | collective-permute-start | bytes 589832 | tf_op jit(solution)/shard_map/while/body/eval_jaxpr/ppermute | solution.py:16
  808.1 19.4 %collective-permute-done.1 = bf16[64,1536]{1,0:T(8,128)(2,1)S(1)} collective-permute-done((bf16[64,1536]{1,0:T(8,128)(2,1)}, bf16[64,1536]{1,0:T(8,128)(2,1)S(1)}, u32[]{:S(2)}, u32[]{:S(2)}) %collective-permute-start.1) | collective-permute-done | bytes 196640 | tf_op jit(solution)/shard_map/while/body/eval_jaxpr/ppermute | solution.py:16
  829.2 132.0 %reduce-scatter.2.cloned.1.call-done = f32[128,48]{0,1:T(8,128)} async-done(((f32[128,1536]{0,1:T(8,128)}), f32[128,48]{0,1:T(8,128)}) %reduce-scatter.2.cloned.1.call-update) | async-done | bytes 24592 | tf_op jit(solution)/shard_map/reduce_scatter | solution.py:22
  (427 shorter events, 665.7 us)
Async XLA Ops:
  7.2 73.6 %all-gather.3.cloned.1.call-start = ((), (), s32[]{:S(2)}) async-start(), calls=%async_computation.2 | async-start | bytes 4866048 | tf_op jit(solution)/shard_map/all_gather | solution.py:127
  7.9 953.3 %reduce-scatter.2.cloned.1.call-start = ((), (), s32[]{:S(2)}) async-start(), calls=%async_computation.1 | async-start | bytes 811008 | tf_op jit(solution)/shard_map/reduce_scatter | solution.py:22
  98.5 15.8 %collective-permute-start = (bf16[64,1536]{1,0:T(8,128)(2,1)}, bf16[64,1536]{1,0:T(8,128)(2,1)S(1)}, u32[]{:S(2)}, u32[]{:S(2)}) collective-permute-start(bf16[64,1536]{1,0:T(8,128)(2,1)} %get-tuple-element.1111), channel_id=1, source_target_pairs={{224,0},{0,32},{32,64},{64,96},{96,128},{128,160},{160,192},{192,2... | collective-permute-start | bytes 589832 | tf_op jit(solution)/shard_map/while/body/eval_jaxpr/ppermute | solution.py:16
  115.6 22.5 %collective-permute-start = (bf16[64,1536]{1,0:T(8,128)(2,1)}, bf16[64,1536]{1,0:T(8,128)(2,1)S(1)}, u32[]{:S(2)}, u32[]{:S(2)}) collective-permute-start(bf16[64,1536]{1,0:T(8,128)(2,1)} %get-tuple-element.1111), channel_id=1, source_target_pairs={{224,0},{0,32},{32,64},{64,96},{96,128},{128,160},{160,192},{192,2... | collective-permute-start | bytes 589832 | tf_op jit(solution)/shard_map/while/body/eval_jaxpr/ppermute | solution.py:16
  139.5 22.5 %collective-permute-start = (bf16[64,1536]{1,0:T(8,128)(2,1)}, bf16[64,1536]{1,0:T(8,128)(2,1)S(1)}, u32[]{:S(2)}, u32[]{:S(2)}) collective-permute-start(bf16[64,1536]{1,0:T(8,128)(2,1)} %get-tuple-element.1111), channel_id=1, source_target_pairs={{224,0},{0,32},{32,64},{64,96},{96,128},{128,160},{160,192},{192,2... | collective-permute-start | bytes 589832 | tf_op jit(solution)/shard_map/while/body/eval_jaxpr/ppermute | solution.py:16
  163.4 22.5 %collective-permute-start = (bf16[64,1536]{1,0:T(8,128)(2,1)}, bf16[64,1536]{1,0:T(8,128)(2,1)S(1)}, u32[]{:S(2)}, u32[]{:S(2)}) collective-permute-start(bf16[64,1536]{1,0:T(8,128)(2,1)} %get-tuple-element.1111), channel_id=1, source_target_pairs={{224,0},{0,32},{32,64},{64,96},{96,128},{128,160},{160,192},{192,2... | collective-permute-start | bytes 589832 | tf_op jit(solution)/shard_map/while/body/eval_jaxpr/ppermute | solution.py:16
  187.3 22.5 %collective-permute-start = (bf16[64,1536]{1,0:T(8,128)(2,1)}, bf16[64,1536]{1,0:T(8,128)(2,1)S(1)}, u32[]{:S(2)}, u32[]{:S(2)}) collective-permute-start(bf16[64,1536]{1,0:T(8,128)(2,1)} %get-tuple-element.1111), channel_id=1, source_target_pairs={{224,0},{0,32},{32,64},{64,96},{96,128},{128,160},{160,192},{192,2... | collective-permute-start | bytes 589832 | tf_op jit(solution)/shard_map/while/body/eval_jaxpr/ppermute | solution.py:16
  294.2 10.0 %collective-permute-start = (bf16[64,1536]{1,0:T(8,128)(2,1)}, bf16[64,1536]{1,0:T(8,128)(2,1)S(1)}, u32[]{:S(2)}, u32[]{:S(2)}) collective-permute-start(bf16[64,1536]{1,0:T(8,128)(2,1)} %get-tuple-element.1111), channel_id=1, source_target_pairs={{224,0},{0,32},{32,64},{64,96},{96,128},{128,160},{160,192},{192,2... | collective-permute-start | bytes 589832 | tf_op jit(solution)/shard_map/while/body/eval_jaxpr/ppermute | solution.py:16
  305.7 13.8 %collective-permute-start = (bf16[64,1536]{1,0:T(8,128)(2,1)}, bf16[64,1536]{1,0:T(8,128)(2,1)S(1)}, u32[]{:S(2)}, u32[]{:S(2)}) collective-permute-start(bf16[64,1536]{1,0:T(8,128)(2,1)} %get-tuple-element.1111), channel_id=1, source_target_pairs={{224,0},{0,32},{32,64},{64,96},{96,128},{128,160},{160,192},{192,2... | collective-permute-start | bytes 589832 | tf_op jit(solution)/shard_map/while/body/eval_jaxpr/ppermute | solution.py:16
  330.6 21.5 %collective-permute-start = (bf16[64,1536]{1,0:T(8,128)(2,1)}, bf16[64,1536]{1,0:T(8,128)(2,1)S(1)}, u32[]{:S(2)}, u32[]{:S(2)}) collective-permute-start(bf16[64,1536]{1,0:T(8,128)(2,1)} %get-tuple-element.1111), channel_id=1, source_target_pairs={{224,0},{0,32},{32,64},{64,96},{96,128},{128,160},{160,192},{192,2... | collective-permute-start | bytes 589832 | tf_op jit(solution)/shard_map/while/body/eval_jaxpr/ppermute | solution.py:16
  353.5 18.5 %collective-permute-start = (bf16[64,1536]{1,0:T(8,128)(2,1)}, bf16[64,1536]{1,0:T(8,128)(2,1)S(1)}, u32[]{:S(2)}, u32[]{:S(2)}) collective-permute-start(bf16[64,1536]{1,0:T(8,128)(2,1)} %get-tuple-element.1111), channel_id=1, source_target_pairs={{224,0},{0,32},{32,64},{64,96},{96,128},{128,160},{160,192},{192,2... | collective-permute-start | bytes 589832 | tf_op jit(solution)/shard_map/while/body/eval_jaxpr/ppermute | solution.py:16
  467.6 15.6 %collective-permute-start = (bf16[64,1536]{1,0:T(8,128)(2,1)}, bf16[64,1536]{1,0:T(8,128)(2,1)S(1)}, u32[]{:S(2)}, u32[]{:S(2)}) collective-permute-start(bf16[64,1536]{1,0:T(8,128)(2,1)} %get-tuple-element.1111), channel_id=1, source_target_pairs={{224,0},{0,32},{32,64},{64,96},{96,128},{128,160},{160,192},{192,2... | collective-permute-start | bytes 589832 | tf_op jit(solution)/shard_map/while/body/eval_jaxpr/ppermute | solution.py:16
  485.9 18.9 %collective-permute-start.1 = (bf16[64,1536]{1,0:T(8,128)(2,1)}, bf16[64,1536]{1,0:T(8,128)(2,1)S(1)}, u32[]{:S(2)}, u32[]{:S(2)}) collective-permute-start(bf16[64,1536]{1,0:T(8,128)(2,1)} %get-tuple-element.1134), channel_id=1, source_target_pairs={{32,0},{64,32},{96,64},{128,96},{160,128},{192,160},{224,192},{0,2... | collective-permute-start | bytes 589832 | tf_op jit(solution)/shard_map/while/body/eval_jaxpr/ppermute | solution.py:16
  538.2 11.2 %collective-permute-start.1 = (bf16[64,1536]{1,0:T(8,128)(2,1)}, bf16[64,1536]{1,0:T(8,128)(2,1)S(1)}, u32[]{:S(2)}, u32[]{:S(2)}) collective-permute-start(bf16[64,1536]{1,0:T(8,128)(2,1)} %get-tuple-element.1134), channel_id=1, source_target_pairs={{32,0},{64,32},{96,64},{128,96},{160,128},{192,160},{224,192},{0,2... | collective-permute-start | bytes 589832 | tf_op jit(solution)/shard_map/while/body/eval_jaxpr/ppermute | solution.py:16
  591.0 18.0 %collective-permute-start.1 = (bf16[64,1536]{1,0:T(8,128)(2,1)}, bf16[64,1536]{1,0:T(8,128)(2,1)S(1)}, u32[]{:S(2)}, u32[]{:S(2)}) collective-permute-start(bf16[64,1536]{1,0:T(8,128)(2,1)} %get-tuple-element.1134), channel_id=1, source_target_pairs={{32,0},{64,32},{96,64},{128,96},{160,128},{192,160},{224,192},{0,2... | collective-permute-start | bytes 589832 | tf_op jit(solution)/shard_map/while/body/eval_jaxpr/ppermute | solution.py:16
  609.7 10.3 %collective-permute-start.1 = (bf16[64,1536]{1,0:T(8,128)(2,1)}, bf16[64,1536]{1,0:T(8,128)(2,1)S(1)}, u32[]{:S(2)}, u32[]{:S(2)}) collective-permute-start(bf16[64,1536]{1,0:T(8,128)(2,1)} %get-tuple-element.1134), channel_id=1, source_target_pairs={{32,0},{64,32},{96,64},{128,96},{160,128},{192,160},{224,192},{0,2... | collective-permute-start | bytes 589832 | tf_op jit(solution)/shard_map/while/body/eval_jaxpr/ppermute | solution.py:16
  620.7 10.9 %collective-permute-start.1 = (bf16[64,1536]{1,0:T(8,128)(2,1)}, bf16[64,1536]{1,0:T(8,128)(2,1)S(1)}, u32[]{:S(2)}, u32[]{:S(2)}) collective-permute-start(bf16[64,1536]{1,0:T(8,128)(2,1)} %get-tuple-element.1134), channel_id=1, source_target_pairs={{32,0},{64,32},{96,64},{128,96},{160,128},{192,160},{224,192},{0,2... | collective-permute-start | bytes 589832 | tf_op jit(solution)/shard_map/while/body/eval_jaxpr/ppermute | solution.py:16
  632.4 20.6 %collective-permute-start.1 = (bf16[64,1536]{1,0:T(8,128)(2,1)}, bf16[64,1536]{1,0:T(8,128)(2,1)S(1)}, u32[]{:S(2)}, u32[]{:S(2)}) collective-permute-start(bf16[64,1536]{1,0:T(8,128)(2,1)} %get-tuple-element.1134), channel_id=1, source_target_pairs={{32,0},{64,32},{96,64},{128,96},{160,128},{192,160},{224,192},{0,2... | collective-permute-start | bytes 589832 | tf_op jit(solution)/shard_map/while/body/eval_jaxpr/ppermute | solution.py:16
  664.8 9.9 %collective-permute-start.1 = (bf16[64,1536]{1,0:T(8,128)(2,1)}, bf16[64,1536]{1,0:T(8,128)(2,1)S(1)}, u32[]{:S(2)}, u32[]{:S(2)}) collective-permute-start(bf16[64,1536]{1,0:T(8,128)(2,1)} %get-tuple-element.1134), channel_id=1, source_target_pairs={{32,0},{64,32},{96,64},{128,96},{160,128},{192,160},{224,192},{0,2... | collective-permute-start | bytes 589832 | tf_op jit(solution)/shard_map/while/body/eval_jaxpr/ppermute | solution.py:16
  708.1 10.3 %collective-permute-start.1 = (bf16[64,1536]{1,0:T(8,128)(2,1)}, bf16[64,1536]{1,0:T(8,128)(2,1)S(1)}, u32[]{:S(2)}, u32[]{:S(2)}) collective-permute-start(bf16[64,1536]{1,0:T(8,128)(2,1)} %get-tuple-element.1134), channel_id=1, source_target_pairs={{32,0},{64,32},{96,64},{128,96},{160,128},{192,160},{224,192},{0,2... | collective-permute-start | bytes 589832 | tf_op jit(solution)/shard_map/while/body/eval_jaxpr/ppermute | solution.py:16
  738.3 18.1 %collective-permute-start.1 = (bf16[64,1536]{1,0:T(8,128)(2,1)}, bf16[64,1536]{1,0:T(8,128)(2,1)S(1)}, u32[]{:S(2)}, u32[]{:S(2)}) collective-permute-start(bf16[64,1536]{1,0:T(8,128)(2,1)} %get-tuple-element.1134), channel_id=1, source_target_pairs={{32,0},{64,32},{96,64},{128,96},{160,128},{192,160},{224,192},{0,2... | collective-permute-start | bytes 589832 | tf_op jit(solution)/shard_map/while/body/eval_jaxpr/ppermute | solution.py:16
  766.1 14.9 %collective-permute-start.1 = (bf16[64,1536]{1,0:T(8,128)(2,1)}, bf16[64,1536]{1,0:T(8,128)(2,1)S(1)}, u32[]{:S(2)}, u32[]{:S(2)}) collective-permute-start(bf16[64,1536]{1,0:T(8,128)(2,1)} %get-tuple-element.1134), channel_id=1, source_target_pairs={{32,0},{64,32},{96,64},{128,96},{160,128},{192,160},{224,192},{0,2... | collective-permute-start | bytes 589832 | tf_op jit(solution)/shard_map/while/body/eval_jaxpr/ppermute | solution.py:16
  790.7 15.2 %collective-permute-start.1 = (bf16[64,1536]{1,0:T(8,128)(2,1)}, bf16[64,1536]{1,0:T(8,128)(2,1)S(1)}, u32[]{:S(2)}, u32[]{:S(2)}) collective-permute-start(bf16[64,1536]{1,0:T(8,128)(2,1)} %get-tuple-element.1134), channel_id=1, source_target_pairs={{32,0},{64,32},{96,64},{128,96},{160,128},{192,160},{224,192},{0,2... | collective-permute-start | bytes 589832 | tf_op jit(solution)/shard_map/while/body/eval_jaxpr/ppermute | solution.py:16
  806.6 20.9 %collective-permute-start.1 = (bf16[64,1536]{1,0:T(8,128)(2,1)}, bf16[64,1536]{1,0:T(8,128)(2,1)S(1)}, u32[]{:S(2)}, u32[]{:S(2)}) collective-permute-start(bf16[64,1536]{1,0:T(8,128)(2,1)} %get-tuple-element.1134), channel_id=1, source_target_pairs={{32,0},{64,32},{96,64},{128,96},{160,128},{192,160},{224,192},{0,2... | collective-permute-start | bytes 589832 | tf_op jit(solution)/shard_map/while/body/eval_jaxpr/ppermute | solution.py:16
  (61 other events, 219.9 us)
Sparse Core Ops, SparseCore 0:
  9.9 70.9 all-gather.2
  829.3 131.8 reduce-scatter.1
where the time goes:
time: 972 us; the launch traced here: 970 us
  waiting for transfers between devices  508 us (52%)
  starting transfers between devices  201 us (21%)
  matrix products  133 us (14%)
  other arithmetic  61.9 us (6%)
  local copies, waits for them, and re-layouts  50.3 us (5%)
  between operations  14.1 us (1%)
    ppermute x38, waiting for transfers between devices, from_behind(): return lax.ppermute(block, axis, route)  306 us
    ppermute x38, starting transfers between devices, from_behind(): return lax.ppermute(block, axis, route)  201 us
    reduce_scatter x1, waiting for transfers between devices, in_one_piece(): out = lax.psum_scatter(both, axis, scatter_dimension=dim, tiled=True)  132 us
    all_gather x1, waiting for transfers between devices, local(): layer_weight = lax.all_gather(frozen_weight[0], 'dp', axis=0, tiled=True)  68.9 us
    dot_general x8, matrix products, forward_layer_pass(): jnp.dot(normalized_hidden, layer_weight, preferred_element_type=jnp.float32)  32.5 us
    dot_general x8, matrix products, backward_layer_pass(): lax.dot_general(preactivation_gradient, layer_weight, (((1,), (1,)), ((),...  31.2 us
  transfers between devices with their start and end apart: 40, of which 40 were waited for; matrix products, arithmetic and copies ran while one was open for 0% of the time, Pallas kernels for 0%

commit v1 on v0

--- a/solution.py
+++ b/solution.py
@@ -124,7 +124,9 @@
 ):
     sections = lax.axis_size("section")
     position = lax.axis_index("section")
-    layer_weight = lax.all_gather(frozen_weight[0], "dp", axis=0, tiled=True)
+    layer_weight = jnp.concatenate(
+        lax.all_to_all(jnp.stack([frozen_weight[0]] * lax.axis_size("dp")), "dp", 0, 0), axis=0
+    )
     down_weight_rows = adapter_down_weight[0]
     up_weight_rows = adapter_up_weight[0]
     gain_row = layer_norm_gain[0]

time: 972 us -> 1020 us (1.049)
  waiting for transfers between devices: 508 us -> 543 us
    all_to_all x0 -> x1, waiting for transfers between devices: none -> 105 us  [local(): lax.all_to_all(jnp.stack([frozen_weight[0]] * lax.axis_size('dp')), 'dp',...]
    all_gather x1 -> x0, waiting for transfers between devices: 68.9 us -> none  [local(): layer_weight = lax.all_gather(frozen_weight[0], 'dp', axis=0, tiled=True)]
    another operation x28 -> x29, local copies, waits for them, and re-layouts: 17.4 us -> 21 us
where the time goes in v1:
time: 1020 us
  waiting for transfers between devices  543 us (53%)
  starting transfers between devices  210 us (21%)
  matrix products  132 us (13%)
  other arithmetic  61.7 us (6%)
  local copies, waits for them, and re-layouts  54.4 us (5%)
  between operations  14.1 us (1%)
    ppermute x38, waiting for transfers between devices, from_behind(): return lax.ppermute(block, axis, route)  306 us
    ppermute x38, starting transfers between devices, from_behind(): return lax.ppermute(block, axis, route)  200 us
    reduce_scatter x1, waiting for transfers between devices, in_one_piece(): out = lax.psum_scatter(both, axis, scatter_dimension=dim, tiled=True)  132 us
    all_to_all x1, waiting for transfers between devices, local(): lax.all_to_all(jnp.stack([frozen_weight[0]] * lax.axis_size('dp')), 'dp',...  105 us
    dot_general x8, matrix products, forward_layer_pass(): jnp.dot(normalized_hidden, layer_weight, preferred_element_type=jnp.float32)  32.8 us
    dot_general x8, matrix products, backward_layer_pass(): lax.dot_general(preactivation_gradient, layer_weight, (((1,), (1,)), ((),...  31.2 us
  transfers between devices with their start and end apart: 40, of which 40 were waited for; matrix products, arithmetic and copies ran while one was open for 0% of the time, Pallas kernels for 0%

profile of v1, /device:TPU:6, one launch (start us, length us, event | category | flops | bytes accessed | tf_op | source)
XLA Modules:
  0.0 1016.6 jit_solution(15272132870546261002)
XLA Ops:
  22.9 104.8 %all-to-all-done = bf16[32,48,1536]{2,1,0:T(8,128)(2,1)} async-done(((bf16[32,48,1536]{2,1,0:T(8,128)(2,1)}), bf16[32,48,1536]{2,1,0:T(8,128)(2,1)}, u32[]{:S(2)}, u32[]{:S(2)}) %all-to-all-start) | async-done | bytes 4718624 | tf_op jit(solution)/shard_map/all_to_all | solution.py:128
  133.7 397.6 %while.42 = (s32[]{:T(128)}, bf16[64,1536]{1,0:T(8,128)(2,1)}, bf16[2,4,64,1536]{3,2,1,0:T(8,128)(2,1)S(1)}, bf16[2,4,64,1536]{3,2,1,0:T(8,128)(2,1)}, bf16[2,4,...) while((s32[]{:T(128)}, bf16[64,1536]{1,0:T(8,128)(2,1)}, ...), condition=%wide.region_4.5_spmd, body=%wide.region_0.4_spmd.sunk | while | flops 332176448 | bytes 21725468 | solution.py:232
  161.3 19.1 %collective-permute-start = (bf16[64,1536]{1,0:T(8,128)(2,1)}, bf16[64,1536]{1,0:T(8,128)(2,1)S(1)}, u32[]{:S(2)}, u32[]{:S(2)}) collective-permute-start(bf16[64,1536]{1,0:T(8,128)(2,1)} %get-tuple-element.1111), channel_id=1, source_target_pairs={{224,0},{0,32},{32,64},{64,96},{96,128},{128,160},{160,192},{192,2... | collective-permute-start | bytes 589832 | tf_op jit(solution)/shard_map/while/body/eval_jaxpr/ppermute | solution.py:16
  185.3 19.1 %collective-permute-start = (bf16[64,1536]{1,0:T(8,128)(2,1)}, bf16[64,1536]{1,0:T(8,128)(2,1)S(1)}, u32[]{:S(2)}, u32[]{:S(2)}) collective-permute-start(bf16[64,1536]{1,0:T(8,128)(2,1)} %get-tuple-element.1111), channel_id=1, source_target_pairs={{224,0},{0,32},{32,64},{64,96},{96,128},{128,160},{160,192},{192,2... | collective-permute-start | bytes 589832 | tf_op jit(solution)/shard_map/while/body/eval_jaxpr/ppermute | solution.py:16
  209.3 19.1 %collective-permute-start = (bf16[64,1536]{1,0:T(8,128)(2,1)}, bf16[64,1536]{1,0:T(8,128)(2,1)S(1)}, u32[]{:S(2)}, u32[]{:S(2)}) collective-permute-start(bf16[64,1536]{1,0:T(8,128)(2,1)} %get-tuple-element.1111), channel_id=1, source_target_pairs={{224,0},{0,32},{32,64},{64,96},{96,128},{128,160},{160,192},{192,2... | collective-permute-start | bytes 589832 | tf_op jit(solution)/shard_map/while/body/eval_jaxpr/ppermute | solution.py:16
  239.3 15.9 %collective-permute-done = bf16[64,1536]{1,0:T(8,128)(2,1)S(1)} collective-permute-done((bf16[64,1536]{1,0:T(8,128)(2,1)}, bf16[64,1536]{1,0:T(8,128)(2,1)S(1)}, u32[]{:S(2)}, u32[]{:S(2)}) %collective-permute-start) | collective-permute-done | bytes 196640 | tf_op jit(solution)/shard_map/while/body/eval_jaxpr/ppermute | solution.py:16
  255.9 13.8 %conditional.4 = (bf16[64,1536]{1,0:T(8,128)(2,1)}, bf16[2,4,64,1536]{3,2,1,0:T(8,128)(2,1)S(1)}, bf16[2,4,64,1536]{3,2,1,0:T(8,128)(2,1)}, bf16[2,4,64,64]{3,2,...) conditional(s32[]{:T(128)} %convert_element_type.177, ...), branch_computations={%region_1.1_spmd, %region_2.3_spmd} | conditional | flops 332176448 | bytes 20152056 | solution.py:219
  279.3 13.8 %conditional.4 = (bf16[64,1536]{1,0:T(8,128)(2,1)}, bf16[2,4,64,1536]{3,2,1,0:T(8,128)(2,1)S(1)}, bf16[2,4,64,1536]{3,2,1,0:T(8,128)(2,1)}, bf16[2,4,64,64]{3,2,...) conditional(s32[]{:T(128)} %convert_element_type.177, ...), branch_computations={%region_1.1_spmd, %region_2.3_spmd} | conditional | flops 332176448 | bytes 20152056 | solution.py:219
  303.4 13.8 %conditional.4 = (bf16[64,1536]{1,0:T(8,128)(2,1)}, bf16[2,4,64,1536]{3,2,1,0:T(8,128)(2,1)S(1)}, bf16[2,4,64,1536]{3,2,1,0:T(8,128)(2,1)}, bf16[2,4,64,64]{3,2,...) conditional(s32[]{:T(128)} %convert_element_type.177, ...), branch_computations={%region_1.1_spmd, %region_2.3_spmd} | conditional | flops 332176448 | bytes 20152056 | solution.py:219
  327.1 13.8 %conditional.4 = (bf16[64,1536]{1,0:T(8,128)(2,1)}, bf16[2,4,64,1536]{3,2,1,0:T(8,128)(2,1)S(1)}, bf16[2,4,64,1536]{3,2,1,0:T(8,128)(2,1)}, bf16[2,4,64,64]{3,2,...) conditional(s32[]{:T(128)} %convert_element_type.177, ...), branch_computations={%region_1.1_spmd, %region_2.3_spmd} | conditional | flops 332176448 | bytes 20152056 | solution.py:219
  377.3 15.7 %collective-permute-start = (bf16[64,1536]{1,0:T(8,128)(2,1)}, bf16[64,1536]{1,0:T(8,128)(2,1)S(1)}, u32[]{:S(2)}, u32[]{:S(2)}) collective-permute-start(bf16[64,1536]{1,0:T(8,128)(2,1)} %get-tuple-element.1111), channel_id=1, source_target_pairs={{224,0},{0,32},{32,64},{64,96},{96,128},{128,160},{160,192},{192,2... | collective-permute-start | bytes 589832 | tf_op jit(solution)/shard_map/while/body/eval_jaxpr/ppermute | solution.py:16
  403.9 15.0 %collective-permute-done = bf16[64,1536]{1,0:T(8,128)(2,1)S(1)} collective-permute-done((bf16[64,1536]{1,0:T(8,128)(2,1)}, bf16[64,1536]{1,0:T(8,128)(2,1)S(1)}, u32[]{:S(2)}, u32[]{:S(2)}) %collective-permute-start) | collective-permute-done | bytes 196640 | tf_op jit(solution)/shard_map/while/body/eval_jaxpr/ppermute | solution.py:16
  419.6 13.9 %conditional.4 = (bf16[64,1536]{1,0:T(8,128)(2,1)}, bf16[2,4,64,1536]{3,2,1,0:T(8,128)(2,1)S(1)}, bf16[2,4,64,1536]{3,2,1,0:T(8,128)(2,1)}, bf16[2,4,64,64]{3,2,...) conditional(s32[]{:T(128)} %convert_element_type.177, ...), branch_computations={%region_1.1_spmd, %region_2.3_spmd} | conditional | flops 332176448 | bytes 20152056 | solution.py:219
  443.7 13.9 %conditional.4 = (bf16[64,1536]{1,0:T(8,128)(2,1)}, bf16[2,4,64,1536]{3,2,1,0:T(8,128)(2,1)S(1)}, bf16[2,4,64,1536]{3,2,1,0:T(8,128)(2,1)}, bf16[2,4,64,64]{3,2,...) conditional(s32[]{:T(128)} %convert_element_type.177, ...), branch_computations={%region_1.1_spmd, %region_2.3_spmd} | conditional | flops 332176448 | bytes 20152056 | solution.py:219
  467.6 13.9 %conditional.4 = (bf16[64,1536]{1,0:T(8,128)(2,1)}, bf16[2,4,64,1536]{3,2,1,0:T(8,128)(2,1)S(1)}, bf16[2,4,64,1536]{3,2,1,0:T(8,128)(2,1)}, bf16[2,4,64,64]{3,2,...) conditional(s32[]{:T(128)} %convert_element_type.177, ...), branch_computations={%region_1.1_spmd, %region_2.3_spmd} | conditional | flops 332176448 | bytes 20152056 | solution.py:219
  491.4 13.8 %conditional.4 = (bf16[64,1536]{1,0:T(8,128)(2,1)}, bf16[2,4,64,1536]{3,2,1,0:T(8,128)(2,1)S(1)}, bf16[2,4,64,1536]{3,2,1,0:T(8,128)(2,1)}, bf16[2,4,64,64]{3,2,...) conditional(s32[]{:T(128)} %convert_element_type.177, ...), branch_computations={%region_1.1_spmd, %region_2.3_spmd} | conditional | flops 332176448 | bytes 20152056 | solution.py:219
  514.8 12.2 %collective-permute-start = (bf16[64,1536]{1,0:T(8,128)(2,1)}, bf16[64,1536]{1,0:T(8,128)(2,1)S(1)}, u32[]{:S(2)}, u32[]{:S(2)}) collective-permute-start(bf16[64,1536]{1,0:T(8,128)(2,1)} %get-tuple-element.1111), channel_id=1, source_target_pairs={{224,0},{0,32},{32,64},{64,96},{96,128},{128,160},{160,192},{192,2... | collective-permute-start | bytes 589832 | tf_op jit(solution)/shard_map/while/body/eval_jaxpr/ppermute | solution.py:16
  532.6 341.8 %while.43 = (s32[]{:T(128)}, bf16[64,1536]{1,0:T(8,128)(2,1)S(1)}, f32[64,1536]{1,0:T(8,128)S(1)}, f32[64,1536]{1,0:T(8,128)S(1)}, s32[]{:T(128)}, /*index=5*/pr...) while((s32[]{:T(128)}, bf16[64,1536]{1,0:T(8,128)(2,1)S(1)}, ...), condition=%wide.region_10.11_spmd, body=%wide.region_5.10_spmd.sunk | while | flops 356265024 | bytes 13259635 | solution.py:291
  533.3 19.2 %collective-permute-done.1 = bf16[64,1536]{1,0:T(8,128)(2,1)S(1)} collective-permute-done((bf16[64,1536]{1,0:T(8,128)(2,1)}, bf16[64,1536]{1,0:T(8,128)(2,1)S(1)}, u32[]{:S(2)}, u32[]{:S(2)}) %collective-permute-start.1) | collective-permute-done | bytes 196640 | tf_op jit(solution)/shard_map/while/body/eval_jaxpr/ppermute | solution.py:16
  640.0 12.1 %collective-permute-start.1 = (bf16[64,1536]{1,0:T(8,128)(2,1)}, bf16[64,1536]{1,0:T(8,128)(2,1)S(1)}, u32[]{:S(2)}, u32[]{:S(2)}) collective-permute-start(bf16[64,1536]{1,0:T(8,128)(2,1)} %get-tuple-element.1134), channel_id=1, source_target_pairs={{32,0},{64,32},{96,64},{128,96},{160,128},{192,160},{224,192},{0,2... | collective-permute-start | bytes 589832 | tf_op jit(solution)/shard_map/while/body/eval_jaxpr/ppermute | solution.py:16
  686.8 13.9 %collective-permute-done.1 = bf16[64,1536]{1,0:T(8,128)(2,1)S(1)} collective-permute-done((bf16[64,1536]{1,0:T(8,128)(2,1)}, bf16[64,1536]{1,0:T(8,128)(2,1)S(1)}, u32[]{:S(2)}, u32[]{:S(2)}) %collective-permute-start.1) | collective-permute-done | bytes 196640 | tf_op jit(solution)/shard_map/while/body/eval_jaxpr/ppermute | solution.py:16
  784.8 12.3 %collective-permute-start.1 = (bf16[64,1536]{1,0:T(8,128)(2,1)}, bf16[64,1536]{1,0:T(8,128)(2,1)S(1)}, u32[]{:S(2)}, u32[]{:S(2)}) collective-permute-start(bf16[64,1536]{1,0:T(8,128)(2,1)} %get-tuple-element.1134), channel_id=1, source_target_pairs={{32,0},{64,32},{96,64},{128,96},{160,128},{192,160},{224,192},{0,2... | collective-permute-start | bytes 589832 | tf_op jit(solution)/shard_map/while/body/eval_jaxpr/ppermute | solution.py:16
  853.8 20.6 %collective-permute-done.1 = bf16[64,1536]{1,0:T(8,128)(2,1)S(1)} collective-permute-done((bf16[64,1536]{1,0:T(8,128)(2,1)}, bf16[64,1536]{1,0:T(8,128)(2,1)S(1)}, u32[]{:S(2)}, u32[]{:S(2)}) %collective-permute-start.1) | collective-permute-done | bytes 196640 | tf_op jit(solution)/shard_map/while/body/eval_jaxpr/ppermute | solution.py:16
  876.1 132.1 %reduce-scatter.2.cloned.1.call-done = f32[128,48]{0,1:T(8,128)} async-done(((f32[128,1536]{0,1:T(8,128)}), f32[128,48]{0,1:T(8,128)}) %reduce-scatter.2.cloned.1.call-update) | async-done | bytes 24592 | tf_op jit(solution)/shard_map/reduce_scatter | solution.py:22
  (435 shorter events, 679.2 us)
Async XLA Ops:
  10.9 116.8 %all-to-all-start = ((bf16[32,48,1536]{2,1,0:T(8,128)(2,1)}), bf16[32,48,1536]{2,1,0:T(8,128)(2,1)}, u32[]{:S(2)}, u32[]{:S(2)}) async-start(bf16[32,48,1536]{2,1,0:T(8,128)(2,1)} %stack.3), calls=%async_computation | async-start | bytes 9437184 | tf_op jit(solution)/shard_map/all_to_all | solution.py:128
  21.0 987.3 %reduce-scatter.2.cloned.1.call-start = ((), (), s32[]{:S(2)}) async-start(), calls=%async_computation.2 | async-start | bytes 811008 | tf_op jit(solution)/shard_map/reduce_scatter | solution.py:22
  144.6 15.3 %collective-permute-start = (bf16[64,1536]{1,0:T(8,128)(2,1)}, bf16[64,1536]{1,0:T(8,128)(2,1)S(1)}, u32[]{:S(2)}, u32[]{:S(2)}) collective-permute-start(bf16[64,1536]{1,0:T(8,128)(2,1)} %get-tuple-element.1111), channel_id=1, source_target_pairs={{224,0},{0,32},{32,64},{64,96},{96,128},{128,160},{160,192},{192,2... | collective-permute-start | bytes 589832 | tf_op jit(solution)/shard_map/while/body/eval_jaxpr/ppermute | solution.py:16
  161.3 22.6 %collective-permute-start = (bf16[64,1536]{1,0:T(8,128)(2,1)}, bf16[64,1536]{1,0:T(8,128)(2,1)S(1)}, u32[]{:S(2)}, u32[]{:S(2)}) collective-permute-start(bf16[64,1536]{1,0:T(8,128)(2,1)} %get-tuple-element.1111), channel_id=1, source_target_pairs={{224,0},{0,32},{32,64},{64,96},{96,128},{128,160},{160,192},{192,2... | collective-permute-start | bytes 589832 | tf_op jit(solution)/shard_map/while/body/eval_jaxpr/ppermute | solution.py:16
  185.3 22.6 %collective-permute-start = (bf16[64,1536]{1,0:T(8,128)(2,1)}, bf16[64,1536]{1,0:T(8,128)(2,1)S(1)}, u32[]{:S(2)}, u32[]{:S(2)}) collective-permute-start(bf16[64,1536]{1,0:T(8,128)(2,1)} %get-tuple-element.1111), channel_id=1, source_target_pairs={{224,0},{0,32},{32,64},{64,96},{96,128},{128,160},{160,192},{192,2... | collective-permute-start | bytes 589832 | tf_op jit(solution)/shard_map/while/body/eval_jaxpr/ppermute | solution.py:16
  209.3 22.6 %collective-permute-start = (bf16[64,1536]{1,0:T(8,128)(2,1)}, bf16[64,1536]{1,0:T(8,128)(2,1)S(1)}, u32[]{:S(2)}, u32[]{:S(2)}) collective-permute-start(bf16[64,1536]{1,0:T(8,128)(2,1)} %get-tuple-element.1111), channel_id=1, source_target_pairs={{224,0},{0,32},{32,64},{64,96},{96,128},{128,160},{160,192},{192,2... | collective-permute-start | bytes 589832 | tf_op jit(solution)/shard_map/while/body/eval_jaxpr/ppermute | solution.py:16
  233.3 21.9 %collective-permute-start = (bf16[64,1536]{1,0:T(8,128)(2,1)}, bf16[64,1536]{1,0:T(8,128)(2,1)S(1)}, u32[]{:S(2)}, u32[]{:S(2)}) collective-permute-start(bf16[64,1536]{1,0:T(8,128)(2,1)} %get-tuple-element.1111), channel_id=1, source_target_pairs={{224,0},{0,32},{32,64},{64,96},{96,128},{128,160},{160,192},{192,2... | collective-permute-start | bytes 589832 | tf_op jit(solution)/shard_map/while/body/eval_jaxpr/ppermute | solution.py:16
  351.2 15.0 %collective-permute-start = (bf16[64,1536]{1,0:T(8,128)(2,1)}, bf16[64,1536]{1,0:T(8,128)(2,1)S(1)}, u32[]{:S(2)}, u32[]{:S(2)}) collective-permute-start(bf16[64,1536]{1,0:T(8,128)(2,1)} %get-tuple-element.1111), channel_id=1, source_target_pairs={{224,0},{0,32},{32,64},{64,96},{96,128},{128,160},{160,192},{192,2... | collective-permute-start | bytes 589832 | tf_op jit(solution)/shard_map/while/body/eval_jaxpr/ppermute | solution.py:16
  377.3 19.2 %collective-permute-start = (bf16[64,1536]{1,0:T(8,128)(2,1)}, bf16[64,1536]{1,0:T(8,128)(2,1)S(1)}, u32[]{:S(2)}, u32[]{:S(2)}) collective-permute-start(bf16[64,1536]{1,0:T(8,128)(2,1)} %get-tuple-element.1111), channel_id=1, source_target_pairs={{224,0},{0,32},{32,64},{64,96},{96,128},{128,160},{160,192},{192,2... | collective-permute-start | bytes 589832 | tf_op jit(solution)/shard_map/while/body/eval_jaxpr/ppermute | solution.py:16
  397.9 21.0 %collective-permute-start = (bf16[64,1536]{1,0:T(8,128)(2,1)}, bf16[64,1536]{1,0:T(8,128)(2,1)S(1)}, u32[]{:S(2)}, u32[]{:S(2)}) collective-permute-start(bf16[64,1536]{1,0:T(8,128)(2,1)} %get-tuple-element.1111), channel_id=1, source_target_pairs={{224,0},{0,32},{32,64},{64,96},{96,128},{128,160},{160,192},{192,2... | collective-permute-start | bytes 589832 | tf_op jit(solution)/shard_map/while/body/eval_jaxpr/ppermute | solution.py:16
  433.4 9.6 collective-permute-start
  514.8 15.7 %collective-permute-start = (bf16[64,1536]{1,0:T(8,128)(2,1)}, bf16[64,1536]{1,0:T(8,128)(2,1)S(1)}, u32[]{:S(2)}, u32[]{:S(2)}) collective-permute-start(bf16[64,1536]{1,0:T(8,128)(2,1)} %get-tuple-element.1111), channel_id=1, source_target_pairs={{224,0},{0,32},{32,64},{64,96},{96,128},{128,160},{160,192},{192,2... | collective-permute-start | bytes 589832 | tf_op jit(solution)/shard_map/while/body/eval_jaxpr/ppermute | solution.py:16
  533.3 19.2 %collective-permute-start.1 = (bf16[64,1536]{1,0:T(8,128)(2,1)}, bf16[64,1536]{1,0:T(8,128)(2,1)S(1)}, u32[]{:S(2)}, u32[]{:S(2)}) collective-permute-start(bf16[64,1536]{1,0:T(8,128)(2,1)} %get-tuple-element.1134), channel_id=1, source_target_pairs={{32,0},{64,32},{96,64},{128,96},{160,128},{192,160},{224,192},{0,2... | collective-permute-start | bytes 589832 | tf_op jit(solution)/shard_map/while/body/eval_jaxpr/ppermute | solution.py:16
  564.2 11.3 %collective-permute-start.1 = (bf16[64,1536]{1,0:T(8,128)(2,1)}, bf16[64,1536]{1,0:T(8,128)(2,1)S(1)}, u32[]{:S(2)}, u32[]{:S(2)}) collective-permute-start(bf16[64,1536]{1,0:T(8,128)(2,1)} %get-tuple-element.1134), channel_id=1, source_target_pairs={{32,0},{64,32},{96,64},{128,96},{160,128},{192,160},{224,192},{0,2... | collective-permute-start | bytes 589832 | tf_op jit(solution)/shard_map/while/body/eval_jaxpr/ppermute | solution.py:16
  587.3 11.5 %collective-permute-start.1 = (bf16[64,1536]{1,0:T(8,128)(2,1)}, bf16[64,1536]{1,0:T(8,128)(2,1)S(1)}, u32[]{:S(2)}, u32[]{:S(2)}) collective-permute-start(bf16[64,1536]{1,0:T(8,128)(2,1)} %get-tuple-element.1134), channel_id=1, source_target_pairs={{32,0},{64,32},{96,64},{128,96},{160,128},{192,160},{224,192},{0,2... | collective-permute-start | bytes 589832 | tf_op jit(solution)/shard_map/while/body/eval_jaxpr/ppermute | solution.py:16
  640.0 17.6 %collective-permute-start.1 = (bf16[64,1536]{1,0:T(8,128)(2,1)}, bf16[64,1536]{1,0:T(8,128)(2,1)S(1)}, u32[]{:S(2)}, u32[]{:S(2)}) collective-permute-start(bf16[64,1536]{1,0:T(8,128)(2,1)} %get-tuple-element.1134), channel_id=1, source_target_pairs={{32,0},{64,32},{96,64},{128,96},{160,128},{192,160},{224,192},{0,2... | collective-permute-start | bytes 589832 | tf_op jit(solution)/shard_map/while/body/eval_jaxpr/ppermute | solution.py:16
  668.5 12.5 %collective-permute-start.1 = (bf16[64,1536]{1,0:T(8,128)(2,1)}, bf16[64,1536]{1,0:T(8,128)(2,1)S(1)}, u32[]{:S(2)}, u32[]{:S(2)}) collective-permute-start(bf16[64,1536]{1,0:T(8,128)(2,1)} %get-tuple-element.1134), channel_id=1, source_target_pairs={{32,0},{64,32},{96,64},{128,96},{160,128},{192,160},{224,192},{0,2... | collective-permute-start | bytes 589832 | tf_op jit(solution)/shard_map/while/body/eval_jaxpr/ppermute | solution.py:16
  681.7 19.1 %collective-permute-start.1 = (bf16[64,1536]{1,0:T(8,128)(2,1)}, bf16[64,1536]{1,0:T(8,128)(2,1)S(1)}, u32[]{:S(2)}, u32[]{:S(2)}) collective-permute-start(bf16[64,1536]{1,0:T(8,128)(2,1)} %get-tuple-element.1134), channel_id=1, source_target_pairs={{32,0},{64,32},{96,64},{128,96},{160,128},{192,160},{224,192},{0,2... | collective-permute-start | bytes 589832 | tf_op jit(solution)/shard_map/while/body/eval_jaxpr/ppermute | solution.py:16
  712.5 9.6 collective-permute-start.1
  755.2 9.6 collective-permute-start.1
  784.8 17.3 %collective-permute-start.1 = (bf16[64,1536]{1,0:T(8,128)(2,1)}, bf16[64,1536]{1,0:T(8,128)(2,1)S(1)}, u32[]{:S(2)}, u32[]{:S(2)}) collective-permute-start(bf16[64,1536]{1,0:T(8,128)(2,1)} %get-tuple-element.1134), channel_id=1, source_target_pairs={{32,0},{64,32},{96,64},{128,96},{160,128},{192,160},{224,192},{0,2... | collective-permute-start | bytes 589832 | tf_op jit(solution)/shard_map/while/body/eval_jaxpr/ppermute | solution.py:16
  811.8 14.9 %collective-permute-start.1 = (bf16[64,1536]{1,0:T(8,128)(2,1)}, bf16[64,1536]{1,0:T(8,128)(2,1)S(1)}, u32[]{:S(2)}, u32[]{:S(2)}) collective-permute-start(bf16[64,1536]{1,0:T(8,128)(2,1)} %get-tuple-element.1134), channel_id=1, source_target_pairs={{32,0},{64,32},{96,64},{128,96},{160,128},{192,160},{224,192},{0,2... | collective-permute-start | bytes 589832 | tf_op jit(solution)/shard_map/while/body/eval_jaxpr/ppermute | solution.py:16
  836.3 16.7 %collective-permute-start.1 = (bf16[64,1536]{1,0:T(8,128)(2,1)}, bf16[64,1536]{1,0:T(8,128)(2,1)S(1)}, u32[]{:S(2)}, u32[]{:S(2)}) collective-permute-start(bf16[64,1536]{1,0:T(8,128)(2,1)} %get-tuple-element.1134), channel_id=1, source_target_pairs={{32,0},{64,32},{96,64},{128,96},{160,128},{192,160},{224,192},{0,2... | collective-permute-start | bytes 589832 | tf_op jit(solution)/shard_map/while/body/eval_jaxpr/ppermute | solution.py:16
  853.7 20.7 %collective-permute-start.1 = (bf16[64,1536]{1,0:T(8,128)(2,1)}, bf16[64,1536]{1,0:T(8,128)(2,1)S(1)}, u32[]{:S(2)}, u32[]{:S(2)}) collective-permute-start(bf16[64,1536]{1,0:T(8,128)(2,1)} %get-tuple-element.1134), channel_id=1, source_target_pairs={{32,0},{64,32},{96,64},{128,96},{160,128},{192,160},{224,192},{0,2... | collective-permute-start | bytes 589832 | tf_op jit(solution)/shard_map/while/body/eval_jaxpr/ppermute | solution.py:16
  (65 other events, 272.5 us)
Sparse Core Ops, SparseCore 0:
  876.3 131.9 reduce-scatter.1
